TPU v7x, 32 devices: a whole 2x2x4 slice. The times are simulated.
32 devices in a mesh: px: 4 (over z), py: 8 (over y, x, core).
Axes of the slice: x: 2, y: 2, z: 4, core: 2. Of those that a mesh axis runs over, the one named last changes fastest.
Arguments:
- stiffness: float32 [9, 3, 3, 64, 1024], P(None, None, None, 'px', 'py'), may hold values from -3 to 9, as said below
- basis: float32 [32, 3, 64, 1024], P(None, None, 'px', 'py'), may hold values from -6 to 6
- current: float32 [3, 64, 1024], P(None, 'px', 'py'), may hold values from -12 to 12, as said below
Outputs:
- new_vectors: float32 [3, 3, 64, 1024], P(None, None, 'px', 'py')
- coefficients: float32 [3, 36], replicated
Inputs may be any that keep to these rules, and one draw needn't show every extreme that they name: `stiffness`: diagonal blocks of the centre coupling dominate each row. `current`: entries of order one.
All inputs are finite; a program needn't handle non-finite values.
Results may differ from a plain program's by a relative error of at most 0.0003.
Values sent between devices are 32-bit elements; how exact they have to be, the bound alone decides.
A program may use at most 64 MiB of HBM per device.

v0:
```python
import jax
import jax.numpy as jnp
from jax import lax
from jax.sharding import PartitionSpec as P

STEPS = 3


EPSILON = 1e-06


def with_halo(shard, sides, width):
    for axis, dim in sides:
        devices, length = (lax.axis_size(axis), shard.shape[dim])
        up = [(i, (i + 1) % devices) for i in range(devices - 1)]
        down = [(j, i) for i, j in up]
        last = lax.slice_in_dim(shard, length - width, length, axis=dim)
        initial = lax.slice_in_dim(shard, 0, width, axis=dim)
        before = lax.ppermute(last, axis, up)
        after = lax.ppermute(initial, axis, down)
        shard = jnp.concatenate([before, shard, after], axis=dim)
    return shard


def stencil(padded, stiffness):
    height = padded.shape[1] - 2
    breadth = padded.shape[2] - 2
    total = jnp.zeros((3, height, breadth), jnp.float32)
    for shift_x in range(3):
        for shift_y in range(3):
            shifted = padded[:, shift_x : shift_x + height, shift_y : shift_y + breadth]
            total = total + jnp.sum(stiffness[shift_x * 3 + shift_y] * shifted[None], axis=1)
    return total


def per_device(stiffness, basis, current):
    degrees = 3.0 * current.shape[1] * current.shape[2] * lax.axis_size("px") * lax.axis_size("py")
    count = basis.shape[0]
    records = []
    betas = []
    settled = []
    pending = current
    for step in range(STEPS):
        padded = with_halo(pending, (("px", 1), ("py", 2)), 1)
        image = stencil(padded, stiffness)
        local_new = [jnp.sum(member * image) for member in settled] + [jnp.sum(pending * image)]
        local_dots = jnp.concatenate(
            [
                jnp.einsum("mabc,abc->m", basis, image, precision=lax.Precision.HIGHEST),
                jnp.stack(local_new),
            ]
        )
        dots, square = lax.psum((local_dots, jnp.sum(pending * pending)), ("px", "py"))
        dots = dots / degrees
        if step == 0:
            scale = jnp.ones((), jnp.float32)
        else:
            scale = jnp.sqrt(square / degrees + EPSILON)
            betas.append(scale)
        vector = pending / scale
        settled.append(vector)
        weights = jnp.concatenate([dots[:-1] / scale, dots[-1:] / (scale * scale)])
        records.append(weights)
        subtract_image = image / scale
        result = subtract_image - jnp.einsum(
            "m,mabc->abc", weights[:count], basis, precision=lax.Precision.HIGHEST
        )
        for place in range(len(settled)):
            result = result - weights[count + place] * settled[place]
        pending = result
    square = lax.psum(jnp.sum(pending * pending), ("px", "py"))
    scale = jnp.sqrt(square / degrees + EPSILON)
    betas.append(scale)
    settled.append(pending / scale)
    produced = settled[1:]
    rows = []
    for step in range(STEPS):
        rows.append(
            jnp.concatenate(
                [records[step], betas[step][None], jnp.zeros((STEPS - 1 - step,), jnp.float32)]
            )
        )
    return (jnp.stack(produced), jnp.stack(rows))


def solution(mesh):
    in_specs = (P(None, None, None, "px", "py"), P(None, None, "px", "py"), P(None, "px", "py"))
    out_specs = (P(None, None, "px", "py"), P())
    return jax.shard_map(
        per_device, mesh=mesh, in_specs=in_specs, out_specs=out_specs, check_vma=False
    )
```

profile of v0, /device:TPU:0, one launch (start us, length us, event | category | flops | bytes accessed | tf_op | source)
XLA Modules:
  0.0 237.2 jit_solution(16599239941670386635)
XLA Ops:
  0.7 0.8 fusion.55
  1.5 1.3 collective-permute-start.1
  2.8 5.6 %collective-permute-start = (f32[3,1,128]{2,1,0:T(1,128)S(1)}, f32[3,1,128]{2,1,0:T(1,128)S(1)}, u32[]{:S(2)}, u32[]{:S(2)}) collective-permute-start(f32[3,1,128]{2,1,0:T(1,128)S(1)} %get-tuple-element.89), channel_id=1, source_target_pairs={{0,8},{8,16},{16,24},{1,9},{9,17},{17,25},{2,10},{10,18},{18,26},{... | collective-permute-start | bytes 4616 | tf_op jit(solution)/shard_map/ppermute | solution.py:19
  8.4 1.3 collective-permute-done
  9.7 0.7 pad_maximum_fusion.4
  10.5 1.3 collective-permute-start.3
  11.8 3.0 %collective-permute-start.2 = (f32[3,18,1]{2,1,0:T(8,128)S(1)}, f32[3,18,1]{2,1,0:T(8,128)S(1)}, u32[]{:S(2)}, u32[]{:S(2)}) collective-permute-start(f32[3,18,1]{2,1,0:T(8,128)S(1)} %get-tuple-element.69), channel_id=1, source_target_pairs={{0,1},{1,2},{2,3},{3,4},{4,5},{5,6},{6,7},{8,9},{9,10},{10,11},{11... | collective-permute-start | bytes 656 | tf_op jit(solution)/shard_map/ppermute | solution.py:19
  14.8 0.8 pad_maximum_fusion.11
  15.7 0.9 pad_maximum_fusion
  16.7 0.6 copy-done.2
  17.4 0.6 multiply_reduce_fusion.8
  18.0 0.8 convolution_bitcast_fusion.2
  18.9 0.7 pad_maximum_fusion.14
  19.6 43.6 %psum.42 = f32[33]{0:T(128)S(1)} all-reduce(f32[33]{0:T(128)S(1)} %pad_maximum_fusion.14), channel_id=1, replica_groups=mesh['px'=4,'py'=8] {'px','py'}, use_global_device_ids=true, to_apply=%region_10.0 | all-reduce | flops 33 | bytes 264 | tf_op jit(solution)/shard_map/psum | solution.py:53
  63.2 0.6 slice.233
  63.8 0.7 fusion.6
  64.5 0.7 multiply_subtract_fusion.2
  65.1 1.3 collective-permute-start.5
  66.4 4.5 %collective-permute-start.4 = (f32[3,1,128]{2,1,0:T(1,128)S(1)}, f32[3,1,128]{2,1,0:T(1,128)S(1)}, u32[]{:S(2)}, u32[]{:S(2)}) collective-permute-start(f32[3,1,128]{2,1,0:T(1,128)S(1)} %get-tuple-element.85), channel_id=1, source_target_pairs={{0,8},{8,16},{16,24},{1,9},{9,17},{17,25},{2,10},{10,18},{18,26},{... | collective-permute-start | bytes 4616 | tf_op jit(solution)/shard_map/ppermute | solution.py:19
  71.0 1.3 collective-permute-done.4
  72.4 1.3 collective-permute-start.7
  73.7 3.0 %collective-permute-start.6 = (f32[3,18,1]{2,1,0:T(8,128)S(1)}, f32[3,18,1]{2,1,0:T(8,128)S(1)}, u32[]{:S(2)}, u32[]{:S(2)}) collective-permute-start(f32[3,18,1]{2,1,0:T(8,128)S(1)} %get-tuple-element.67), channel_id=1, source_target_pairs={{0,1},{1,2},{2,3},{3,4},{4,5},{5,6},{6,7},{8,9},{9,10},{10,11},{11... | collective-permute-start | bytes 656 | tf_op jit(solution)/shard_map/ppermute | solution.py:19
  76.7 0.8 collective-permute-done.6
  77.8 0.7 multiply_reduce_fusion.7
  78.5 0.8 convolution_bitcast_fusion.1
  79.4 1.4 pad_maximum_fusion.15
  80.8 44.0 %all-reduce.1 = (f32[34]{0:T(128)S(1)}, f32[]{:T(128)}) all-reduce(f32[34]{0:T(128)S(1)} %pad_maximum_fusion.15, f32[]{:T(128)} %get-tuple-element.33), channel_id=1, replica_groups=mesh['px'=4,'py'=8] {'px','py'}, use_global_device_ids=true, to_apply=%region_24.0 | all-reduce | flops 35 | bytes 280 | tf_op jit(solution)/shard_map/psum | solution.py:53
  125.5 0.6 slice.249
  126.1 0.6 slice.248
  126.7 0.7 fusion.3
  128.0 0.6 multiply_subtract_fusion.1
  128.6 1.3 collective-permute-start.9
  129.9 4.5 %collective-permute-start.8 = (f32[3,1,128]{2,1,0:T(1,128)S(1)}, f32[3,1,128]{2,1,0:T(1,128)S(1)}, u32[]{:S(2)}, u32[]{:S(2)}) collective-permute-start(f32[3,1,128]{2,1,0:T(1,128)S(1)} %get-tuple-element.81), channel_id=1, source_target_pairs={{0,8},{8,16},{16,24},{1,9},{9,17},{17,25},{2,10},{10,18},{18,26},{... | collective-permute-start | bytes 4616 | tf_op jit(solution)/shard_map/ppermute | solution.py:19
  134.6 1.2 collective-permute-done.8
  135.9 1.3 collective-permute-start.11
  137.2 3.0 %collective-permute-start.10 = (f32[3,18,1]{2,1,0:T(8,128)S(1)}, f32[3,18,1]{2,1,0:T(8,128)S(1)}, u32[]{:S(2)}, u32[]{:S(2)}) collective-permute-start(f32[3,18,1]{2,1,0:T(8,128)S(1)} %get-tuple-element.65), channel_id=1, source_target_pairs={{0,1},{1,2},{2,3},{3,4},{4,5},{5,6},{6,7},{8,9},{9,10},{10,11},{11... | collective-permute-start | bytes 656 | tf_op jit(solution)/shard_map/ppermute | solution.py:19
  140.2 0.8 collective-permute-done.10
  141.3 0.7 multiply_reduce_fusion.4
  142.0 0.8 convolution_bitcast_fusion
  142.9 1.9 pad_maximum_fusion.16
  144.8 44.1 %all-reduce = (f32[35]{0:T(128)S(1)}, f32[]{:T(128)}) all-reduce(f32[35]{0:T(128)S(1)} %pad_maximum_fusion.16, f32[]{:T(128)} %get-tuple-element.29), channel_id=1, replica_groups=mesh['px'=4,'py'=8] {'px','py'}, use_global_device_ids=true, to_apply=%region_39.0 | all-reduce | flops 36 | bytes 288 | tf_op jit(solution)/shard_map/psum | solution.py:53
  189.5 0.6 slice.266
  190.1 0.7 fusion.56
  190.8 0.7 fusion
  192.1 1.9 multiply_reduce_fusion
  194.0 41.2 %psum.47 = f32[]{:T(128)} all-reduce(f32[]{:T(128)} %get-tuple-element.40), channel_id=1, replica_groups=mesh['px'=4,'py'=8] {'px','py'}, use_global_device_ids=true, to_apply=%region_41.0 | all-reduce | flops 1 | bytes 8 | tf_op jit(solution)/shard_map/psum | solution.py:71
  236.0 0.6 pad_maximum_fusion.3
  236.6 0.6 pad_maximum_fusion.13
  (41 shorter events, 1.3 us)
Async XLA Ops:
  0.6 17.4 %copy-start = (f32[32,3,16,128]{3,2,1,0:T(8,128)S(1)}, f32[32,3,16,128]{3,2,1,0:T(8,128)}, u32[]{:S(2)}) copy-start(f32[32,3,16,128]{3,2,1,0:T(8,128)} %param.4) | copy-start | bytes 2359300
  0.6 16.1 %copy-start.1 = (f32[9,3,3,16,128]{4,3,2,1,0:T(8,128)S(1)}, f32[9,3,3,16,128]{4,3,2,1,0:T(8,128)}, u32[]{:S(2)}) copy-start(f32[9,3,3,16,128]{4,3,2,1,0:T(8,128)} %param.3) | copy-start | bytes 1990660
  1.5 6.9 %collective-permute-start.1 = (f32[3,1,128]{2,1,0:T(1,128)S(1)}, f32[3,1,128]{2,1,0:T(1,128)S(1)}, u32[]{:S(2)}, u32[]{:S(2)}) collective-permute-start(f32[3,1,128]{2,1,0:T(1,128)S(1)} %get-tuple-element.88), channel_id=1, source_target_pairs={{8,0},{16,8},{24,16},{9,1},{17,9},{25,17},{10,2},{18,10},{26,18},{... | collective-permute-start | bytes 4616 | tf_op jit(solution)/shard_map/ppermute | solution.py:20
  2.8 6.9 %collective-permute-start = (f32[3,1,128]{2,1,0:T(1,128)S(1)}, f32[3,1,128]{2,1,0:T(1,128)S(1)}, u32[]{:S(2)}, u32[]{:S(2)}) collective-permute-start(f32[3,1,128]{2,1,0:T(1,128)S(1)} %get-tuple-element.89), channel_id=1, source_target_pairs={{0,8},{8,16},{16,24},{1,9},{9,17},{17,25},{2,10},{10,18},{18,26},{... | collective-permute-start | bytes 4616 | tf_op jit(solution)/shard_map/ppermute | solution.py:19
  10.5 5.2 %collective-permute-start.3 = (f32[3,18,1]{2,1,0:T(8,128)S(1)}, f32[3,18,1]{2,1,0:T(8,128)S(1)}, u32[]{:S(2)}, u32[]{:S(2)}) collective-permute-start(f32[3,18,1]{2,1,0:T(8,128)S(1)} %get-tuple-element.68), channel_id=1, source_target_pairs={{1,0},{2,1},{3,2},{4,3},{5,4},{6,5},{7,6},{9,8},{10,9},{11,10},{12... | collective-permute-start | bytes 656 | tf_op jit(solution)/shard_map/ppermute | solution.py:20
  11.8 3.9 %collective-permute-start.2 = (f32[3,18,1]{2,1,0:T(8,128)S(1)}, f32[3,18,1]{2,1,0:T(8,128)S(1)}, u32[]{:S(2)}, u32[]{:S(2)}) collective-permute-start(f32[3,18,1]{2,1,0:T(8,128)S(1)} %get-tuple-element.69), channel_id=1, source_target_pairs={{0,1},{1,2},{2,3},{3,4},{4,5},{5,6},{6,7},{8,9},{9,10},{10,11},{11... | collective-permute-start | bytes 656 | tf_op jit(solution)/shard_map/ppermute | solution.py:19
  16.6 0.7 copy-start.2
  65.1 5.9 %collective-permute-start.5 = (f32[3,1,128]{2,1,0:T(1,128)S(1)}, f32[3,1,128]{2,1,0:T(1,128)S(1)}, u32[]{:S(2)}, u32[]{:S(2)}) collective-permute-start(f32[3,1,128]{2,1,0:T(1,128)S(1)} %get-tuple-element.84), channel_id=1, source_target_pairs={{8,0},{16,8},{24,16},{9,1},{17,9},{25,17},{10,2},{18,10},{26,18},{... | collective-permute-start | bytes 4616 | tf_op jit(solution)/shard_map/ppermute | solution.py:20
  66.4 5.8 %collective-permute-start.4 = (f32[3,1,128]{2,1,0:T(1,128)S(1)}, f32[3,1,128]{2,1,0:T(1,128)S(1)}, u32[]{:S(2)}, u32[]{:S(2)}) collective-permute-start(f32[3,1,128]{2,1,0:T(1,128)S(1)} %get-tuple-element.85), channel_id=1, source_target_pairs={{0,8},{8,16},{16,24},{1,9},{9,17},{17,25},{2,10},{10,18},{18,26},{... | collective-permute-start | bytes 4616 | tf_op jit(solution)/shard_map/ppermute | solution.py:19
  72.4 4.4 %collective-permute-start.7 = (f32[3,18,1]{2,1,0:T(8,128)S(1)}, f32[3,18,1]{2,1,0:T(8,128)S(1)}, u32[]{:S(2)}, u32[]{:S(2)}) collective-permute-start(f32[3,18,1]{2,1,0:T(8,128)S(1)} %get-tuple-element.66), channel_id=1, source_target_pairs={{1,0},{2,1},{3,2},{4,3},{5,4},{6,5},{7,6},{9,8},{10,9},{11,10},{12... | collective-permute-start | bytes 656 | tf_op jit(solution)/shard_map/ppermute | solution.py:20
  73.7 3.9 %collective-permute-start.6 = (f32[3,18,1]{2,1,0:T(8,128)S(1)}, f32[3,18,1]{2,1,0:T(8,128)S(1)}, u32[]{:S(2)}, u32[]{:S(2)}) collective-permute-start(f32[3,18,1]{2,1,0:T(8,128)S(1)} %get-tuple-element.67), channel_id=1, source_target_pairs={{0,1},{1,2},{2,3},{3,4},{4,5},{5,6},{6,7},{8,9},{9,10},{10,11},{11... | collective-permute-start | bytes 656 | tf_op jit(solution)/shard_map/ppermute | solution.py:19
  128.6 5.9 %collective-permute-start.9 = (f32[3,1,128]{2,1,0:T(1,128)S(1)}, f32[3,1,128]{2,1,0:T(1,128)S(1)}, u32[]{:S(2)}, u32[]{:S(2)}) collective-permute-start(f32[3,1,128]{2,1,0:T(1,128)S(1)} %get-tuple-element.80), channel_id=1, source_target_pairs={{8,0},{16,8},{24,16},{9,1},{17,9},{25,17},{10,2},{18,10},{26,18},{... | collective-permute-start | bytes 4616 | tf_op jit(solution)/shard_map/ppermute | solution.py:20
  129.9 5.8 %collective-permute-start.8 = (f32[3,1,128]{2,1,0:T(1,128)S(1)}, f32[3,1,128]{2,1,0:T(1,128)S(1)}, u32[]{:S(2)}, u32[]{:S(2)}) collective-permute-start(f32[3,1,128]{2,1,0:T(1,128)S(1)} %get-tuple-element.81), channel_id=1, source_target_pairs={{0,8},{8,16},{16,24},{1,9},{9,17},{17,25},{2,10},{10,18},{18,26},{... | collective-permute-start | bytes 4616 | tf_op jit(solution)/shard_map/ppermute | solution.py:19
  135.9 4.4 %collective-permute-start.11 = (f32[3,18,1]{2,1,0:T(8,128)S(1)}, f32[3,18,1]{2,1,0:T(8,128)S(1)}, u32[]{:S(2)}, u32[]{:S(2)}) collective-permute-start(f32[3,18,1]{2,1,0:T(8,128)S(1)} %get-tuple-element.64), channel_id=1, source_target_pairs={{1,0},{2,1},{3,2},{4,3},{5,4},{6,5},{7,6},{9,8},{10,9},{11,10},{12... | collective-permute-start | bytes 656 | tf_op jit(solution)/shard_map/ppermute | solution.py:20
  137.2 3.9 %collective-permute-start.10 = (f32[3,18,1]{2,1,0:T(8,128)S(1)}, f32[3,18,1]{2,1,0:T(8,128)S(1)}, u32[]{:S(2)}, u32[]{:S(2)}) collective-permute-start(f32[3,18,1]{2,1,0:T(8,128)S(1)} %get-tuple-element.65), channel_id=1, source_target_pairs={{0,1},{1,2},{2,3},{3,4},{4,5},{5,6},{6,7},{8,9},{9,10},{10,11},{11... | collective-permute-start | bytes 656 | tf_op jit(solution)/shard_map/ppermute | solution.py:19
where the time goes:
time: 238 us; the launch traced here: 237 us
  blocking collectives  173 us (73%)
  starting transfers between devices  31.5 us (13%)
  other arithmetic  13.6 us (6%)
  waiting for transfers between devices  5.4 us (2%)
  local copies, waits for them, and re-layouts  5.01 us (2%)
  matrix products  4.49 us (2%)
  between operations  4.26 us (2%)
    psum x3, blocking collectives, per_device(): lax.psum((local_dots, jnp.sum(pending * pending)), ('px', 'py'))  132 us
    psum x1, blocking collectives, per_device(): square = lax.psum(jnp.sum(pending * pending), ('px', 'py'))  41.2 us
    ppermute x6, starting transfers between devices, with_halo(): before = lax.ppermute(last, axis, up)  23.8 us
    ppermute x6, starting transfers between devices, with_halo(): after = lax.ppermute(initial, axis, down)  7.72 us
    ppermute x6, waiting for transfers between devices, with_halo(): before = lax.ppermute(last, axis, up)  5.38 us
  transfers between devices with their start and end apart: 12, of which 5 were waited for; matrix products, arithmetic and copies ran while one was open for 0% of the time, Pallas kernels for 0%

commit v1 on v0

v1 whole, which is shorter than its diff:
```python
import jax
import jax.numpy as jnp
from jax import lax
from jax.experimental import pallas as pl
from jax.experimental.pallas import tpu as pltpu
from jax.sharding import PartitionSpec as P

STEPS = 3
EPSILON = 1e-06
MESH = pl.DeviceIdType.MESH
HIGHEST = lax.Precision.HIGHEST

SENDS = (
    (0, 1, 0, 16),
    (0, -1, 16, 16),
    (1, 1, 32, 8),
    (1, -1, 40, 8),
    (-1, 1, 48, 8),
    (-1, -1, 56, 8),
    (1, 0, 64, 8),
    (-1, 0, 72, 8),
)
COLS = 64
HALO = 80
EXTRA = 96
SQUARE = 120


def iota(shape, dim):
    return lax.broadcasted_iota(jnp.int32, shape, dim)


def kernel(
    count, total_size,
    stiff_hbm, basis_hbm, cur_hbm,
    new_out, coef_out,
    stiff, basis, fld, img, edge, halo_in, halo, vcols, vrows, vh_cols, vh_rows,
    parts, msg, recv,
    load_sem, halo_send, halo_recv, vh_send, vh_recv, msg_send, msg_recv,
):
    nx, ny = lax.axis_size("px"), lax.axis_size("py")
    n = nx * ny
    x, y = lax.axis_index("px"), lax.axis_index("py")
    me = x * ny + y
    rows, width = 16, 128
    fields = 3 * count

    load_cur = pltpu.make_async_copy(cur_hbm, fld.at[0], load_sem.at[0])
    load_basis = pltpu.make_async_copy(basis_hbm, basis, load_sem.at[1])
    load_stiff = pltpu.make_async_copy(stiff_hbm, stiff, load_sem.at[2])
    load_cur.start()
    load_stiff.start()
    load_basis.start()

    halo_in[...] = jnp.zeros_like(halo_in)
    vh_cols[...] = jnp.zeros_like(vh_cols)
    vh_rows[...] = jnp.zeros_like(vh_rows)
    parts[...] = jnp.zeros_like(parts)

    def peer_id(k):
        peer = lax.rem(me + k, n)
        return (lax.div(peer, ny), lax.rem(peer, ny))

    barrier = pltpu.get_barrier_semaphore()

    def greet(k, carry):
        pl.semaphore_signal(barrier, inc=1, device_id=peer_id(k), device_id_type=MESH)
        return carry

    lax.fori_loop(1, n, greet, 0)

    row16, lane16 = iota((rows, width), 0), iota((rows, width), 1)
    row8, lane8 = iota((8, width), 0), iota((8, width), 1)

    def pack_edges(read, slot):
        packed = jnp.zeros((rows, width), jnp.float32)
        lines = jnp.zeros((8, width), jnp.float32)
        for a in range(3):
            f = read(a)
            packed = jnp.where(lane16 == a, pltpu.roll(f, a + 1, 1), packed)
            packed = jnp.where(lane16 == 3 + a, pltpu.roll(f, 3 + a, 1), packed)
            lines = jnp.where(row8 == a, jnp.broadcast_to(f[rows - 1 :, :], (8, width)), lines)
            lines = jnp.where(row8 == 3 + a, jnp.broadcast_to(f[0:1, :], (8, width)), lines)
        edge[slot, 0:rows, :] = packed
        edge[slot, rows : rows + 8, :] = lines

    def present(dx, dy):
        return (x + dx >= 0) & (x + dx < nx) & (y + dy >= 0) & (y + dy < ny)

    def halo_copy(slot, i):
        dx, dy, at, size = SENDS[i]
        first = rows if at >= COLS else (8 if dx == 1 else 0)
        return pltpu.make_async_remote_copy(
            src_ref=edge.at[slot, pl.ds(first, size), :],
            dst_ref=halo_in.at[slot, pl.ds(at, size), :],
            send_sem=halo_send.at[slot, i],
            recv_sem=halo_recv.at[slot, i],
            device_id=(x + dx, y + dy),
            device_id_type=MESH,
        )

    def vh_copy(i):
        dx, dy, at, size = SENDS[i]
        if at >= COLS:
            side = 0 if dx == 1 else 1
            src = vrows.at[side]
            dst = vh_rows.at[side, pl.ds(0, fields), :]
        else:
            side = 0 if dy == 1 else 1
            src = vcols.at[side, pl.ds(8 if dx == 1 else 0, size), :]
            dst = vh_cols.at[pl.ds(at, size), :]
        return pltpu.make_async_remote_copy(
            src_ref=src, dst_ref=dst, send_sem=vh_send.at[i], recv_sem=vh_recv.at[i],
            device_id=(x + dx, y + dy), device_id_type=MESH,
        )

    def start_all(make):
        for i, (dx, dy, _, _) in enumerate(SENDS):
            @pl.when(present(dx, dy))
            def _():
                make(i).start()

    def wait_recv_all(make):
        for i, (dx, dy, _, _) in enumerate(SENDS):
            @pl.when(present(-dx, -dy))
            def _():
                make(i).wait_recv()

    def wait_send_all(make):
        for i, (dx, dy, _, _) in enumerate(SENDS):
            @pl.when(present(dx, dy))
            def _():
                make(i).wait_send()

    load_cur.wait()
    pack_edges(lambda a: fld[0, a], 0)
    pl.semaphore_wait(barrier, n - 1)
    start_all(lambda i: halo_copy(0, i))

    load_basis.wait()
    vrows[0] = basis[pl.ds(rows - 1, fields, stride=rows), :]
    vrows[1] = basis[pl.ds(0, fields, stride=rows), :]
    last_cols = jnp.zeros((rows, width), jnp.float32)
    first_cols = jnp.zeros((rows, width), jnp.float32)
    for k in range(fields):
        f = basis[k * rows : (k + 1) * rows, :]
        last_cols = jnp.where(lane16 == k, pltpu.roll(f, (k + 1) % width, 1), last_cols)
        first_cols = jnp.where(lane16 == k, pltpu.roll(f, k, 1) if k else f, first_cols)
    vcols[0] = last_cols
    vcols[1] = first_cols
    start_all(vh_copy)
    load_stiff.wait()

    def message_copy(s, k):
        return pltpu.make_async_remote_copy(
            src_ref=msg.at[s, pl.ds(0, 1), :],
            dst_ref=recv.at[s, pl.ds(me, 1), :],
            send_sem=msg_send.at[s],
            recv_sem=msg_recv.at[s],
            device_id=peer_id(k),
            device_id_type=MESH,
        )

    def send_message(s):
        folded = parts[pl.ds(0, width, stride=8), :]
        for j in range(1, 8):
            folded = folded + parts[pl.ds(j, width, stride=8), :]
        sums = lax.dot_general(
            jnp.ones((8, width), jnp.float32), folded, (((1,), (1,)), ((), ())),
            precision=HIGHEST, preferred_element_type=jnp.float32,
        )
        msg[s] = sums
        recv[s, pl.ds(me, 1), :] = sums[0:1]

        def send(k, carry):
            message_copy(s, k).start()
            return carry

        lax.fori_loop(1, n, send, 0)

    def wait_message(s):
        pltpu.make_async_copy(
            recv.at[s, pl.ds(0, n - 1), :], recv.at[s, pl.ds(0, n - 1), :], msg_recv.at[s]
        ).wait()
        summed = jnp.sum(recv[s], axis=0, keepdims=True) / total_size
        return jnp.broadcast_to(summed, (8, width))

    def fold(values):
        total = values[0]
        for value in values[1:]:
            total = total + value
        return total[0:8] + total[8:16]

    def splat(row, lane):
        return jnp.broadcast_to(row[:, lane : lane + 1], (8, width))

    def twice(tile):
        return jnp.concatenate([tile, tile], axis=0)

    def stencil(s):
        left, right = halo[s, 0:16, :], halo[s, 16:32, :]

        def around(f, above, below):
            up = jnp.where(row16 == 0, jnp.broadcast_to(above, f.shape), pltpu.roll(f, 1, 0))
            down = jnp.where(row16 == rows - 1, jnp.broadcast_to(below, f.shape), pltpu.roll(f, rows - 1, 0))
            return (up, f, down)

        lefts = around(left, halo[s, 39:40, :], halo[s, 48:49, :])
        rights = around(right, halo[s, 47:48, :], halo[s, 56:57, :])
        image = [jnp.zeros((rows, width), jnp.float32) for _ in range(3)]
        for b in range(3):
            moved = around(fld[s, b], halo[s, 64 + b : 65 + b, :], halo[s, 75 + b : 76 + b, :])
            for i in range(3):
                f = moved[i]
                l = pltpu.roll(lefts[i], width - b, 1) if b else lefts[i]
                r = pltpu.roll(rights[i], width - 4 - b, 1)
                west = jnp.where(lane16 == 0, l, pltpu.roll(f, 1, 1))
                east = jnp.where(lane16 == width - 1, r, pltpu.roll(f, width - 1, 1))
                for j, g in enumerate((west, f, east)):
                    for a in range(3):
                        image[a] = image[a] + stiff[3 * i + j, a, b] * g
        return image

    wait_recv_all(lambda i: halo_copy(0, i))
    halo[0] = halo_in[0]

    rows_out = []
    betas = []
    for s in range(STEPS):
        image = stencil(s)
        for a in range(3):
            img[a] = image[a]
        if s < STEPS - 1:
            pack_edges(lambda a: img[a], s + 1)
            start_all(lambda i, s=s: halo_copy(s + 1, i))
        for m in range(count):
            part = fold([basis[(3 * m + a) * rows : (3 * m + a + 1) * rows, :] * img[a] for a in range(3)])
            for a in range(3):
                parts[(3 * m + a) * 8 : (3 * m + a + 1) * 8, :] = part
        for k in range(s + 1):
            parts[(EXTRA + k) * 8 : (EXTRA + k + 1) * 8, :] = fold([fld[k, a] * img[a] for a in range(3)])
        parts[SQUARE * 8 : SQUARE * 8 + 8, :] = fold([fld[s, a] * fld[s, a] for a in range(3)])
        send_message(s)
        if s == 0:
            wait_recv_all(vh_copy)
        if s < STEPS - 1:
            wait_recv_all(lambda i, s=s: halo_copy(s + 1, i))
        dots = wait_message(s)

        if s == 0:
            inverse = jnp.ones((8, width), jnp.float32)
        else:
            beta = jnp.sqrt(splat(dots, SQUARE) + EPSILON)
            betas.append(beta)
            inverse = 1.0 / beta
            for a in range(3):
                vector = fld[s, a] * twice(inverse)
                fld[s, a] = vector
                new_out[s - 1, a] = vector
            if s < STEPS - 1:
                halo[s] = halo[s] * inverse[0:1]
        weights = dots * inverse
        weights = jnp.where(lane8 == EXTRA + s, weights * inverse, weights)
        rows_out.append(weights)
        result = [img[a] * twice(inverse) for a in range(3)]
        for m in range(count):
            w = twice(splat(weights, 3 * m))
            for a in range(3):
                result[a] = result[a] - w * basis[(3 * m + a) * rows : (3 * m + a + 1) * rows, :]
        for k in range(s + 1):
            w = twice(splat(weights, EXTRA + k))
            for a in range(3):
                result[a] = result[a] - w * fld[k, a]
        for a in range(3):
            fld[s + 1, a] = result[a]
        if s < STEPS - 1:
            sub, lane = iota((width, width), 0), iota((width, width), 1)
            picks = (lax.rem(sub, 3) == lax.rem(lane, 3)) & (sub < 6) & (lane < fields)
            spread = jnp.where(picks, jnp.broadcast_to(weights[0:1], (width, width)), 0.0)
            cols = lax.dot_general(
                vh_cols[...], spread, (((1,), (1,)), ((), ())),
                precision=HIGHEST, preferred_element_type=jnp.float32,
            )
            lines = [
                jnp.dot(spread[0:8], vh_rows[side], precision=HIGHEST, preferred_element_type=jnp.float32)
                for side in range(2)
            ]
            ring = halo_in[s + 1] * inverse[0:1] - jnp.concatenate([cols] + lines, axis=0)
            for k in range(s + 1):
                ring = ring - splat(weights, EXTRA + k)[0:1] * halo[k]
            halo[s + 1] = ring

    parts[SQUARE * 8 : SQUARE * 8 + 8, :] = fold([fld[STEPS, a] * fld[STEPS, a] for a in range(3)])
    send_message(STEPS)
    sub, lane = iota((width, width), 0), iota((width, width), 1)
    gather = jnp.where((sub == 3 * lane) & (lane < count), 1.0, 0.0)
    gather = jnp.where((sub - EXTRA == lane - count) & (lane >= count) & (lane < count + STEPS), 1.0, gather)
    stacked = rows_out[0]
    for s in range(1, STEPS):
        stacked = jnp.where(row8 == s, rows_out[s], stacked)
    stacked = jnp.where((lane8 >= EXTRA) & (lane8 > EXTRA + row8), 0.0, stacked)
    table = jnp.dot(stacked, gather, precision=HIGHEST, preferred_element_type=jnp.float32)
    last = wait_message(STEPS)
    beta = jnp.sqrt(splat(last, SQUARE) + EPSILON)
    betas.append(beta)
    for a in range(3):
        new_out[STEPS - 1, a] = fld[STEPS, a] * twice(1.0 / beta)
    for s in range(STEPS):
        table = jnp.where((row8 == s) & (lane8 == count + 1 + s), betas[s], table)
    coef_out[...] = table[0:STEPS, 0 : count + STEPS + 1]

    for s in range(STEPS):
        wait_send_all(lambda i, s=s: halo_copy(s, i))
    wait_send_all(vh_copy)
    for s in range(STEPS + 1):
        pltpu.make_async_copy(
            recv.at[s, pl.ds(0, n - 1), :], recv.at[s, pl.ds(0, n - 1), :], msg_send.at[s]
        ).wait()


def per_device(stiffness, basis, current):
    count, _, rows, width = basis.shape
    assert (rows, width) == (16, 128) and 3 * count <= EXTRA
    n = lax.axis_size("px") * lax.axis_size("py")
    total_size = 3.0 * rows * width * n
    f32 = jnp.float32
    vmem = pltpu.VMEM
    dma = pltpu.SemaphoreType.DMA

    def body(*refs):
        kernel(count, total_size, *refs)

    return pl.pallas_call(
        body,
        out_shape=(
            jax.ShapeDtypeStruct((STEPS, 3, rows, width), f32),
            jax.ShapeDtypeStruct((STEPS, count + STEPS + 1), f32),
        ),
        in_specs=[pl.BlockSpec(memory_space=pl.ANY)] * 3,
        out_specs=(pl.BlockSpec(memory_space=vmem), pl.BlockSpec(memory_space=vmem)),
        scratch_shapes=[
            vmem(stiffness.shape, f32),
            vmem((3 * count * rows, width), f32),
            vmem((STEPS + 1, 3, rows, width), f32),
            vmem((3, rows, width), f32),
            vmem((STEPS, rows + 8, width), f32),
            vmem((STEPS, HALO, width), f32),
            vmem((STEPS, HALO, width), f32),
            vmem((2, rows, width), f32),
            vmem((2, 3 * count, width), f32),
            vmem((COLS, width), f32),
            vmem((2, width, width), f32),
            vmem((8 * width, width), f32),
            vmem((STEPS + 1, 8, width), f32),
            vmem((STEPS + 1, n, width), f32),
            dma((3,)),
            dma((STEPS, len(SENDS))),
            dma((STEPS, len(SENDS))),
            dma((len(SENDS),)),
            dma((len(SENDS),)),
            dma((STEPS + 1,)),
            dma((STEPS + 1,)),
        ],
        compiler_params=pltpu.CompilerParams(collective_id=0, has_side_effects=True),
        name="arnoldi",
    )(stiffness, basis.reshape(3 * count * rows, width), current)


def solution(mesh):
    in_specs = (P(None, None, None, "px", "py"), P(None, None, "px", "py"), P(None, "px", "py"))
    out_specs = (P(None, None, "px", "py"), P())
    return jax.shard_map(
        per_device, mesh=mesh, in_specs=in_specs, out_specs=out_specs, check_vma=False
    )
```

time: 238 us -> 34.7 us (0.15)
  blocking collectives: 173 us -> 0 us
  Pallas kernels: 0 us -> 31.8 us
  starting transfers between devices: 31.5 us -> 0 us
  other arithmetic: 13.6 us -> 0 us
  waiting for transfers between devices: 5.4 us -> 0 us
  matrix products: 4.49 us -> 0 us
  between operations: 4.26 us -> 0.65 us
  local copies, waits for them, and re-layouts: 5.01 us -> 2.1 us
    psum x4 -> x0, blocking collectives: 173 us -> none  [the longest x3 132 us: per_device(): lax.psum((local_dots, jnp.sum(pending * pending)), ('px', 'py'))]
    pallas_call x0 -> x1, Pallas kernels: none -> 31.8 us  [per_device(): pl.pallas_call(body, out_shape=(jax.ShapeDtypeStruct((STEPS, 3, rows, wid...]
    ppermute x12 -> x0, starting transfers between devices: 31.5 us -> none  [the longest x6 23.8 us: with_halo(): before = lax.ppermute(last, axis, up)]
    concatenate x12 -> x0, other arithmetic: 6.8 us -> none  [the longest x3 4.08 us: per_device(): jnp.concatenate([jnp.einsum('mabc,abc->m', basis, image, precision=lax.Pr...]
    ppermute x12 -> x0, waiting for transfers between devices: 5.4 us -> none  [the longest x6 5.38 us: with_halo(): before = lax.ppermute(last, axis, up)]
    dot_general x6 -> x0, matrix products: 4.49 us -> none  [the longest x3 2.46 us: per_device(): jnp.einsum('mabc,abc->m', basis, image, precision=lax.Precision.HIGHEST)]
    slice x16 -> x0, local copies, waits for them, and re-layouts: 4.37 us -> none  [the longest x3 1.78 us: per_device(): weights = jnp.concatenate([dots[:-1] / scale, dots[-1:] / (scale * scale)])]
    reduce_sum x7 -> x0, other arithmetic: 4.13 us -> none  [the longest x1 1.87 us: per_device(): square = lax.psum(jnp.sum(pending * pending), ('px', 'py'))]
  transfers between devices with their start and end apart: 12 -> 0, of which waited for: 5 -> 0; matrix products, arithmetic and copies ran while one was open for 0% -> 0% of each run, Pallas kernels for 0% -> 0%
where the time goes in v1:
time: 34.7 us; the launch traced here: 34.6 us
  Pallas kernels  31.8 us (92%)
  local copies, waits for them, and re-layouts  2.1 us (6%)
  between operations  0.65 us (2%)
    pallas_call x1, Pallas kernels, per_device(): pl.pallas_call(body, out_shape=(jax.ShapeDtypeStruct((STEPS, 3, rows, wid...  31.8 us
    unnamed x4, local copies, waits for them, and re-layouts  2.1 us

profile of v1, /device:TPU:0, one launch (start us, length us, event | category | flops | bytes accessed | tf_op | source)
XLA Modules:
  0.0 34.6 jit_solution(3257937105338429777)
XLA Ops:
  0.6 31.8 %arnoldi.1 = (f32[3,3,16,128]{3,2,1,0:T(8,128)}, f32[3,36]{1,0:T(4,128)}) custom-call(f32[9,3,3,16,128]{4,3,2,1,0:T(8,128)} %refs_0_.1, f32[1536,128]{1,0:T(8,128)} %bitcast.1, f32[3,16,128]{2,1,0:T(8,128)} %refs_2_.1), custom_call_target="tpu_custom_call" | custom-call | tf_op jit(solution)/shard_map/arnoldi/pallas_call | solution.py:333
  32.4 0.0 copy-start
  32.5 1.5 %copy.7 = f32[3,3,16,128]{3,2,1,0:T(8,128)} copy(f32[3,3,16,128]{3,2,1,0:T(8,128)} %get-tuple-element.4) | data formatting | bytes 147456
  34.0 0.0 copy-done
  34.0 0.6 %copy.8 = f32[3,36]{1,0:T(4,128)} copy(f32[3,36]{1,0:T(4,128)S(1)} %copy-done) | data formatting | bytes 864
Async XLA Ops:
  32.4 1.5 %copy-start = (f32[3,36]{1,0:T(4,128)S(1)}, f32[3,36]{1,0:T(4,128)}, u32[]{:S(2)}) copy-start(f32[3,36]{1,0:T(4,128)} %get-tuple-element.5) | copy-start | bytes 1300

commit v2 on v1

--- a/solution.py
+++ b/solution.py
@@ -57,17 +57,27 @@
     vh_rows[...] = jnp.zeros_like(vh_rows)
     parts[...] = jnp.zeros_like(parts)
 
-    def peer_id(k):
-        peer = lax.rem(me + k, n)
-        return (lax.div(peer, ny), lax.rem(peer, ny))
+    def for_peers(act):
+        def plane(px, first):
+            def one(k, py):
+                py = jnp.where(py == ny - 1, 0, py + 1)
+                act((px, py))
+                return py
+
+            start = y if first else jnp.where(y == 0, ny - 1, y - 1)
+            lax.fori_loop(first, ny, one, start, unroll=min(8, ny) if not first else 1)
+
+        def other(k, px):
+            px = jnp.where(px == nx - 1, 0, px + 1)
+            plane(px, 0)
+            return px
+
+        lax.fori_loop(1, nx, other, x)
+        plane(x, 1)
 
     barrier = pltpu.get_barrier_semaphore()
 
-    def greet(k, carry):
-        pl.semaphore_signal(barrier, inc=1, device_id=peer_id(k), device_id_type=MESH)
-        return carry
-
-    lax.fori_loop(1, n, greet, 0)
+    for_peers(lambda peer: pl.semaphore_signal(barrier, inc=1, device_id=peer, device_id_type=MESH))
 
     row16, lane16 = iota((rows, width), 0), iota((rows, width), 1)
     row8, lane8 = iota((8, width), 0), iota((8, width), 1)
@@ -151,13 +161,13 @@
     start_all(vh_copy)
     load_stiff.wait()
 
-    def message_copy(s, k):
+    def message_copy(s, peer):
         return pltpu.make_async_remote_copy(
             src_ref=msg.at[s, pl.ds(0, 1), :],
             dst_ref=recv.at[s, pl.ds(me, 1), :],
             send_sem=msg_send.at[s],
             recv_sem=msg_recv.at[s],
-            device_id=peer_id(k),
+            device_id=peer,
             device_id_type=MESH,
         )
 
@@ -172,11 +182,7 @@
         msg[s] = sums
         recv[s, pl.ds(me, 1), :] = sums[0:1]
 
-        def send(k, carry):
-            message_copy(s, k).start()
-            return carry
-
-        lax.fori_loop(1, n, send, 0)
+        for_peers(lambda peer: message_copy(s, peer).start())
 
     def wait_message(s):
         pltpu.make_async_copy(
@@ -330,7 +336,7 @@
     def body(*refs):
         kernel(count, total_size, *refs)
 
-    return pl.pallas_call(
+    new, coef = pl.pallas_call(
         body,
         out_shape=(
             jax.ShapeDtypeStruct((STEPS, 3, rows, width), f32),
@@ -365,6 +371,21 @@
         name="arnoldi",
     )(stiffness, basis.reshape(3 * count * rows, width), current)
 
+    def hand_out(new_ref, coef_ref, new_out, coef_out):
+        new_out[...] = new_ref[...]
+        coef_out[...] = coef_ref[...]
+
+    return pl.pallas_call(
+        hand_out,
+        out_shape=(
+            jax.ShapeDtypeStruct(new.shape, f32),
+            jax.ShapeDtypeStruct(coef.shape, f32),
+        ),
+        in_specs=[pl.BlockSpec(memory_space=vmem)] * 2,
+        out_specs=(pl.BlockSpec(memory_space=vmem), pl.BlockSpec(memory_space=vmem)),
+        name="hand_out",
+    )(new, coef)
+
 
 def solution(mesh):
     in_specs = (P(None, None, None, "px", "py"), P(None, None, "px", "py"), P(None, "px", "py"))

time: 34.7 us -> 33.9 us (0.977)
  local copies, waits for them, and re-layouts: 2.1 us -> 0 us
  Pallas kernels: 31.8 us -> 33.1 us
    unnamed x4 -> x0, local copies, waits for them, and re-layouts: 2.1 us -> none
    pallas_call x0 -> x1, Pallas kernels: none -> 1.53 us  [per_device(): pl.pallas_call(hand_out, out_shape=(jax.ShapeDtypeStruct(new.shape, f32),...]
where the time goes in v2:
time: 33.9 us; the launch traced here: 33.8 us
  Pallas kernels  33.1 us (98%)
  between operations  0.64 us (2%)
    pallas_call x1, Pallas kernels, per_device(): pl.pallas_call(body, out_shape=(jax.ShapeDtypeStruct((STEPS, 3, rows, wid...  31.6 us
    pallas_call x1, Pallas kernels, per_device(): pl.pallas_call(hand_out, out_shape=(jax.ShapeDtypeStruct(new.shape, f32),...  1.53 us

profile of v2, /device:TPU:0, one launch (start us, length us, event | category | flops | bytes accessed | tf_op | source)
XLA Modules:
  0.0 33.8 jit_solution(12103255756612788573)
XLA Ops:
  0.6 31.6 %arnoldi.1 = (f32[3,3,16,128]{3,2,1,0:T(8,128)}, f32[3,36]{1,0:T(4,128)}) custom-call(f32[9,3,3,16,128]{4,3,2,1,0:T(8,128)} %refs_0_.1, f32[1536,128]{1,0:T(8,128)} %bitcast.1, f32[3,16,128]{2,1,0:T(8,128)} %refs_2_.1), custom_call_target="tpu_custom_call" | custom-call | tf_op jit(solution)/shard_map/arnoldi/pallas_call | solution.py:339
  32.2 1.5 %hand_out.1 = (f32[3,3,16,128]{3,2,1,0:T(8,128)}, f32[3,36]{1,0:T(4,128)}) custom-call(f32[3,3,16,128]{3,2,1,0:T(8,128)} %get-tuple-element.4.new_ref, f32[3,36]{1,0:T(4,128)} %get-tuple-element.5.coef_ref), custom_call_target="tpu_custom_call" | custom-call | tf_op jit(solution)/shard_map/hand_out/pallas_call | solution.py:378

commit v3 on v2

--- a/solution.py
+++ b/solution.py
@@ -339,8 +339,8 @@
     new, coef = pl.pallas_call(
         body,
         out_shape=(
-            jax.ShapeDtypeStruct((STEPS, 3, rows, width), f32),
-            jax.ShapeDtypeStruct((STEPS, count + STEPS + 1), f32),
+            vmem((STEPS, 3, rows, width), f32),
+            vmem((STEPS, count + STEPS + 1), f32),
         ),
         in_specs=[pl.BlockSpec(memory_space=pl.ANY)] * 3,
         out_specs=(pl.BlockSpec(memory_space=vmem), pl.BlockSpec(memory_space=vmem)),
@@ -371,20 +371,7 @@
         name="arnoldi",
     )(stiffness, basis.reshape(3 * count * rows, width), current)
 
-    def hand_out(new_ref, coef_ref, new_out, coef_out):
-        new_out[...] = new_ref[...]
-        coef_out[...] = coef_ref[...]
-
-    return pl.pallas_call(
-        hand_out,
-        out_shape=(
-            jax.ShapeDtypeStruct(new.shape, f32),
-            jax.ShapeDtypeStruct(coef.shape, f32),
-        ),
-        in_specs=[pl.BlockSpec(memory_space=vmem)] * 2,
-        out_specs=(pl.BlockSpec(memory_space=vmem), pl.BlockSpec(memory_space=vmem)),
-        name="hand_out",
-    )(new, coef)
+    return new, coef
 
 
 def solution(mesh):

time: 33.9 us -> 33 us (0.973)
  Pallas kernels: 33.1 us -> 31 us
  local copies, waits for them, and re-layouts: 0 us -> 1.21 us
    pallas_call x2 -> x1, Pallas kernels: 33.1 us -> 31 us  [per_device(): pl.pallas_call(body, out_shape=(vmem((STEPS, 3, rows, width), f32), vmem(...]
    unnamed x0 -> x2, local copies, waits for them, and re-layouts: none -> 1.21 us
where the time goes in v3:
time: 33 us; the launch traced here: 32.8 us
  Pallas kernels  31 us (94%)
  local copies, waits for them, and re-layouts  1.21 us (4%)
  between operations  0.64 us (2%)
    pallas_call x1, Pallas kernels, per_device(): pl.pallas_call(body, out_shape=(vmem((STEPS, 3, rows, width), f32), vmem(...  31 us
    unnamed x2, local copies, waits for them, and re-layouts  1.21 us

profile of v3, /device:TPU:0, one launch (start us, length us, event | category | flops | bytes accessed | tf_op | source)
XLA Modules:
  0.0 32.8 jit_solution(13449775727810778658)
XLA Ops:
  0.6 31.0 %arnoldi.1 = (f32[3,3,16,128]{3,2,1,0:T(8,128)S(1)}, f32[3,36]{1,0:T(4,128)S(1)}) custom-call(f32[9,3,3,16,128]{4,3,2,1,0:T(8,128)} %refs_0_.1, f32[1536,128]{1,0:T(8,128)} %bitcast.1, f32[3,16,128]{2,1,0:T(8,128)} %refs_2_.1), custom_call_target="tpu_custom_call" | custom-call | tf_op jit(solution)/shard_map/arnoldi/pallas_call | solution.py:339
  31.6 0.6 %copy.7 = f32[3,3,16,128]{3,2,1,0:T(8,128)} copy(f32[3,3,16,128]{3,2,1,0:T(8,128)S(1)} %get-tuple-element.2) | data formatting | bytes 147456
  32.2 0.6 %copy.8 = f32[3,36]{1,0:T(4,128)} copy(f32[3,36]{1,0:T(4,128)S(1)} %get-tuple-element.3) | data formatting | bytes 864
